TPU v7x, 32 devices: a whole 2x2x4 slice. The times are simulated.
32 devices in a mesh: groups: 2 (over x), row: 16 (over z, y, core).
Axes of the slice: x: 2, y: 2, z: 4, core: 2. Of those that a mesh axis runs over, the one named last changes fastest.
Arguments:
- homolog_embedding: bfloat16 [128, 256, 64], P('groups', 'row'), parts along dimension 0, may hold values from -6 to 6
- pair_state_tiles: bfloat16 [512, 256, 128], P(('groups', 'row')), parts along dimension 0, may hold values from -6 to 6
- alignment_mask: int32 [128, 256], P('groups', 'row'), parts along dimension 0, may hold values 0 or 1
- token_real_mask: int32 [512], P('groups'), parts along dimension 0, may hold values 0 or 1
- lineup_standardize_scaling: float32 [64], replicated, may hold values from 0.1 to 1.9
- former_factor_proj: bfloat16 [64, 32], replicated, may hold values from -0.75 to 0.75
- latter_factor_proj: bfloat16 [64, 32], replicated, may hold values from -0.75 to 0.75
- outer_output_weight: bfloat16 [1024, 128], replicated, may hold values from -0.1875 to 0.1875
- pair_norm_gain: float32 [128], replicated, may hold values from 0.1 to 1.9
- pair_logit_weight: float32 [128, 8], replicated
- content_vector_proj: bfloat16 [64, 256], replicated, may hold values from -0.75 to 0.75
- sigmoid_switch_proj: bfloat16 [64, 256], replicated, may hold values from -0.75 to 0.75
- final_result_proj: bfloat16 [256, 64], replicated, may hold values from -0.375 to 0.375
Outputs:
- alignment_updated: bfloat16 [128, 256, 64], P('groups', 'row'), parts along dimension 0
- pair_updated: bfloat16 [512, 256, 128], P(('groups', 'row')), parts along dimension 0
There are 2 independent parts, one for each index of `groups`. A program takes and returns all parts, laid end to end along the dimension named above; an argument that names none is the same for every part. Nothing has to cross between parts.
All inputs are finite; a program needn't handle non-finite values. No bound on the sum of `alignment_mask` on one device may be relied on, other than what follows from the above.
Results may differ from a plain program's by a relative error of at most 0.007.
Values may be sent and summed in bfloat16 or wider, within the bound.
No kernel may reach another device: no remote copies, remote signals or barrier semaphores. Data moves between devices by JAX's collectives and lax.ppermute only.
A program may use at most 128 MiB of HBM per device.

v0:
```python
import jax
import jax.numpy as jnp
from jax import lax
from jax.sharding import PartitionSpec as P


def layer_normalize(inputs, gain):
    inputs = inputs.astype(jnp.float32)
    center = jnp.mean(inputs, axis=-1, keepdims=True)
    spread = jnp.mean((inputs - center) ** 2, axis=-1, keepdims=True)
    return (inputs - center) * lax.rsqrt(spread + 1e-05) * gain


def pair_terms(folded, local_mask, right_piece, mask_piece):
    product = jnp.einsum("seiz,sje->ijz", folded, right_piece, preferred_element_type=jnp.float32)
    counts = jnp.einsum("si,sj->ij", local_mask, mask_piece, preferred_element_type=jnp.float32)
    return product / (1.0 + counts)[:, :, None]


def shards(
    homolog_embedding,
    pair_state_tiles,
    alignment_mask,
    token_real_mask,
    lineup_standardize_scaling,
    former_factor_proj,
    latter_factor_proj,
    outer_output_weight,
    pair_norm_gain,
    pair_logit_weight,
    content_vector_proj,
    sigmoid_switch_proj,
    final_result_proj,
):
    normed_input = layer_normalize(homolog_embedding, lineup_standardize_scaling).astype(
        jnp.bfloat16
    )
    mask_halved = alignment_mask.astype(jnp.bfloat16)
    mask_float = mask_halved.astype(jnp.float32)
    left_rows = (
        jnp.dot(normed_input, former_factor_proj, preferred_element_type=jnp.float32)
        * mask_float[:, :, None]
    ).astype(jnp.bfloat16)
    factor = former_factor_proj.shape[1]
    channels = outer_output_weight.shape[1]
    weight_cube = outer_output_weight.reshape(factor, factor, channels)
    folded = jnp.einsum(
        "sic,cez->seiz", left_rows, weight_cube, preferred_element_type=jnp.float32
    ).astype(jnp.bfloat16)
    head_count = pair_logit_weight.shape[1]
    head_width = content_vector_proj.shape[1] // head_count
    gathered, gathered_mask = (
        lax.all_gather(normed_input, "row", axis=1, tiled=True),
        lax.all_gather(mask_halved, "row", axis=1, tiled=True),
    )
    right_all = (
        jnp.dot(gathered, latter_factor_proj, preferred_element_type=jnp.float32)
        * gathered_mask.astype(jnp.float32)[:, :, None]
    ).astype(jnp.bfloat16)
    update = pair_terms(folded, mask_halved, right_all, gathered_mask)
    pair_updated = (pair_state_tiles.astype(jnp.float32) + update).astype(jnp.bfloat16)
    pair_normed = layer_normalize(pair_updated, pair_norm_gain)
    logits = jnp.einsum(
        "ijc,ch->hij", pair_normed, pair_logit_weight, precision=lax.Precision.HIGHEST
    )
    logits = jnp.where(token_real_mask[None, None, :] == 1, logits, -1000000000.0)
    weights = jax.nn.softmax(logits, axis=2).astype(jnp.bfloat16)
    seq_count, local_tokens = (normed_input.shape[0], normed_input.shape[1])
    values_all = jnp.dot(gathered, content_vector_proj, preferred_element_type=jnp.float32).astype(
        jnp.bfloat16
    )
    span = values_all.shape[1]
    heads_piece = values_all.reshape(seq_count, span, head_count, head_width)
    term = jnp.einsum("hij,sjhc->sihc", weights, heads_piece, preferred_element_type=jnp.float32)
    average = term.reshape(seq_count, local_tokens, head_count * head_width)
    gate_vals = jax.nn.sigmoid(
        jnp.dot(normed_input, sigmoid_switch_proj, preferred_element_type=jnp.float32)
    )
    gated_output = (gate_vals * average).astype(jnp.bfloat16)
    update_alignment = jnp.dot(gated_output, final_result_proj, preferred_element_type=jnp.float32)
    alignment_updated = (homolog_embedding.astype(jnp.float32) + update_alignment).astype(
        jnp.bfloat16
    )
    return (alignment_updated, pair_updated)


def solution(mesh):
    placed = (
        P("groups", "row", None),
        P(("groups", "row"), None, None),
        P("groups", "row"),
        P("groups"),
        P(),
        P(),
        P(),
        P(),
        P(),
        P(),
        P(),
        P(),
        P(),
    )
    return jax.shard_map(
        shards,
        mesh=mesh,
        in_specs=placed,
        out_specs=(P("groups", "row", None), P(("groups", "row"), None, None)),
        check_vma=False,
    )
```

profile of v0, /device:TPU:0, one launch (start us, length us, event | category | flops | bytes accessed | tf_op | source)
XLA Modules:
  0.0 111.5 jit_solution(13931650329398912923)
XLA Ops:
  7.2 0.0 copy-start
  7.2 0.0 copy-start.3
  7.2 0.0 all-gather.2.cloned.1.call-start
  7.2 1.2 %convert_reduce_fusion.1 = f32[64,16]{1,0:T(8,128)S(1)} fusion(bf16[64,16,64]{2,1,0:T(8,128)(2,1)} %param.13), kind=kLoop, calls=%fused_computation.44 | loop fusion | flops 130048 | bytes 135168 | tf_op jit(solution)/shard_map/reduce_sum | solution.py:9
  8.4 1.3 %fusion.44 = f32[64,16]{1,0:T(8,128)S(1)} fusion(bf16[64,16,64]{2,1,0:T(8,128)(2,1)} %param.13, f32[64,16]{1,0:T(8,128)S(1)} %broadcast_multiply_fusion), kind=kLoop, calls=%fused_computation.47 | loop fusion | flops 261120 | bytes 139264 | tf_op jit(solution)/shard_map/reduce_sum | solution.py:10
  9.8 2.0 %fusion.46 = bf16[64,16,64]{2,1,0:T(8,128)(2,1)} fusion(bf16[64,16,64]{2,1,0:T(8,128)(2,1)} %param.13, f32[64]{0:T(128)} %param.17, f32[64,16]{1,0:T(8,128)S(1)} %add_rsqrt_fusion, f32[64,16]{1,0:T(8,128)S(1)} %broadcast_multiply_fusion), kind=kLoop, calls=%fused_computation.49 | loop fusion | flops 327680 | bytes 270592 | tf_op jit(solution)/shard_map/convert_element_type | solution.py:35
  11.8 0.0 all-gather.2.cloned.1.call-update
  11.8 0.7 fusion.62
  12.5 23.4 %all_gather.7 = bf16[64,256]{0,1:T(8,128)(2,1)S(1)} all-gather(bf16[64,16]{0,1:T(8,128)(2,1)S(1)} %get-tuple-element.11), channel_id=1, replica_groups=mesh['groups'=2,'row'=16] {'row'}, dimensions={1}, use_global_device_ids=true | all-gather | bytes 34816 | tf_op jit(solution)/shard_map/all_gather | solution.py:54
  35.9 0.1 copy.47
  36.0 1.5 %copy.46 = bf16[16,256,128]{1,2,0:T(8,128)(2,1)S(1)} copy(bf16[16,256,128]{2,1,0:T(8,128)(2,1)} %param.14) | data formatting | bytes 2097152 | tf_op args[1]
  37.5 0.7 broadcast_compare_fusion
  38.2 0.1 convolution_add_fusion.1
  38.3 0.0 copy-done.3
  38.3 6.0 %convert_bitcast_fusion = bf16[64,32,16,128]{3,0,1,2:T(8,128)(2,1)} fusion(bf16[32,32,128]{2,1,0:T(8,128)(2,1)S(1)} %bitcast.59, bf16[64,16,64]{2,1,0:T(8,128)(2,1)} %fusion.46, f32[64,16]{0,1:T(8,128)S(1)} %get-tuple-element.10, bf16[64,32]{0,1:T(8,128)(2,1)} %param.18), kind=kOutput, calls=%fused_computation.6 | convolution fusion | flops 276889600 | bytes 8790016 | tf_op jit(solution)/shard_map/sic,cez->seiz/dot_general | solution.py:47
  44.3 22.9 %all-gather.2.cloned.1.call-done = bf16[64,256,64]{2,1,0:T(8,128)(2,1)} async-done(((bf16[64,16,64]{2,1,0:T(8,128)(2,1)}), bf16[64,256,64]{2,1,0:T(8,128)(2,1)}) %all-gather.2.cloned.1.call-update) | async-done | bytes 2097168 | tf_op jit(solution)/shard_map/all_gather | solution.py:53
  67.2 3.7 %fusion.19 = bf16[64,256,32,1]{1,2,0,3:T(8,128)(2,1)S(1)} fusion(bf16[64,256,64]{2,1,0:T(8,128)(2,1)} %all-gather.2.cloned.1.call-done, f32[64,256]{1,0:T(8,128)S(1)} %convert_element_type.54, bf16[64,32]{0,1:T(8,128)(2,1)S(1)} %copy-done.5), kind=kOutput, calls=%fused_computation.20 | convolution fusion | flops 68157440 | bytes 3215360 | tf_op jit(solution)/shard_map/dot_general | solution.py:57
  70.9 0.0 copy-start.8
  70.9 11.0 %convert_reduce_fusion = (f32[16,256]{1,0:T(8,128)S(1)}, bf16[16,256,128]{1,2,0:T(8,128)(2,1)S(1)}) fusion(f32[16,256]{1,0:T(8,128)S(1)} %convolution_add_fusion.1, bf16[64,256,32,1]{1,2,0,3:T(8,128)(2,1)S(1)} %fusion.19, bf16[64,32,16,128]{3,0,1,2:T(8,128)(2,1)} %convert_bitcast_fusion, bf16[16,256,128]{1,2,0:T(8,128)(2,1)S(1)} %copy.46), kind=kOutput, calls=%fused_computation.9 | convolution fusion | flops 2150625280 | bytes 11567104 | tf_op jit(solution)/shard_map/seiz,sje->ijz/dot_general | solution.py:15
  82.0 1.3 %copy.57 = bf16[16,256,128]{2,1,0:T(8,128)(2,1)} copy(bf16[16,256,128]{1,2,0:T(8,128)(2,1)S(1)} %get-tuple-element.13) | data formatting | bytes 2097152
  83.3 0.3 fusion.11
  83.7 1.5 %fusion.34 = f32[8,16,256]{2,0,1:T(8,128)S(1)} fusion(bf16[16,256,128]{1,2,0:T(8,128)(2,1)S(1)} %get-tuple-element.13, f32[128]{0:T(128)S(1)} %copy-done.8, f32[16,256]{1,0:T(8,128)S(1)} %add_rsqrt_fusion.1, f32[16,256]{1,0:T(8,128)S(1)} %broadcast_multiply_fusion.1, pred[256]{0:T(512)(128)(4,1)S(1)} %broadcast_compare_fusion, f32[128,8]{0,1:T(8,128)S(1)} %copy-done.7), kind=kOutput, calls=%fused_computation.36 | convolution fusion | flops 52461568 | bytes 1217280 | tf_op jit(solution)/shard_map/ijc,ch->hij/dot_general | solution.py:63
  85.1 0.2 fusion.38
  85.3 0.0 copy-done
  85.3 4.5 %convolution_convert_fusion = bf16[64,256,256]{1,2,0:T(8,128)(2,1)S(1)} fusion(bf16[64,256,64]{2,1,0:T(8,128)(2,1)} %all-gather.2.cloned.1.call-done, bf16[64,256]{1,0:T(8,128)(2,1)S(1)} %copy-done), kind=kOutput, calls=%fused_computation.7 | convolution fusion | flops 541065216 | bytes 10518528 | tf_op jit(solution)/shard_map/dot_general | solution.py:69
  89.9 7.5 %fusion.8 = f32[64,16,8,32]{3,1,0,2:T(8,128)} fusion(bf16[64,256,8,32]{1,3,2,0:T(8,128)(2,1)S(1)} %bitcast.57, bf16[8,16,256,1]{2,0,1,3:T(8,128)(2,1)S(1)} %fusion.38), kind=kOutput, calls=%fused_computation.12 | convolution fusion | flops 134217728 | bytes 9502720 | tf_op jit(solution)/shard_map/hij,sjhc->sihc/dot_general | solution.py:74
  97.4 2.9 %copy.54 = f32[64,16,8,32]{0,3,2,1:T(8,128)S(1)} copy(f32[64,16,8,32]{3,1,0,2:T(8,128)} %fusion.8) | data formatting | bytes 2097152 | tf_op jit(solution)/shard_map/hij,sjhc->sihc/transpose | solution.py:74
  100.3 0.0 copy-start.1
  100.3 0.0 copy-start.4
  100.3 1.6 %copy.55 = f32[64,16,256]{2,0,1:T(8,128)} copy(f32[64,16,256]{0,2,1:T(8,128)S(1)} %bitcast.58) | data formatting | bytes 2097152 | tf_op jit(solution)/shard_map/reshape | solution.py:75
  101.9 1.6 %fusion.24 = bf16[64,16,256]{2,0,1:T(8,128)(2,1)S(1)} fusion(f32[64,16,256]{2,0,1:T(8,128)} %copy.55, bf16[64,16,64]{2,1,0:T(8,128)(2,1)S(1)} %copy-done.2, bf16[64,256]{1,0:T(8,128)(2,1)S(1)} %copy-done.6), kind=kOutput, calls=%fused_computation.26 | convolution fusion | flops 34865152 | bytes 1736704 | tf_op jit(solution)/shard_map/dot_general | solution.py:77
  103.6 1.1 %fusion.25 = bf16[64,16,64]{2,1,0:T(8,128)(2,1)} fusion(bf16[64,16,64]{2,1,0:T(8,128)(2,1)S(1)} %copy-done.1, bf16[64,16,256]{2,0,1:T(8,128)(2,1)S(1)} %fusion.24, bf16[256,64]{0,1:T(8,128)(2,1)S(1)} %copy-done.4), kind=kOutput, calls=%fused_computation.28 | convolution fusion | flops 33751040 | bytes 819200 | tf_op jit(solution)/shard_map/dot_general | solution.py:80
  (16 shorter events, 0.1 us)
Async XLA Ops:
  7.2 78.2 %copy-start = (bf16[64,256]{1,0:T(8,128)(2,1)S(1)}, bf16[64,256]{1,0:T(8,128)(2,1)}, u32[]{:S(2)}) copy-start(bf16[64,256]{1,0:T(8,128)(2,1)} %param.23) | copy-start | bytes 98308
  7.2 31.1 %copy-start.3 = (bf16[1024,128]{1,0:T(8,128)(2,1)S(1)}, bf16[1024,128]{1,0:T(8,128)(2,1)}, u32[]{:S(2)}) copy-start(bf16[1024,128]{1,0:T(8,128)(2,1)} %param.20) | copy-start | bytes 786436
  7.2 60.0 %all-gather.2.cloned.1.call-start = ((), (), s32[]{:S(2)}) async-start(), calls=%async_computation | async-start | bytes 4456448 | tf_op jit(solution)/shard_map/all_gather | solution.py:53
  38.3 28.9 %copy-start.5 = (bf16[64,32]{0,1:T(8,128)(2,1)S(1)}, bf16[64,32]{0,1:T(8,128)(2,1)}, u32[]{:S(2)}) copy-start(bf16[64,32]{0,1:T(8,128)(2,1)} %param.19) | copy-start | bytes 12292
  70.9 12.7 %copy-start.7 = (f32[128,8]{0,1:T(8,128)S(1)}, f32[128,8]{0,1:T(8,128)}, u32[]{:S(2)}) copy-start(f32[128,8]{0,1:T(8,128)} %param.22) | copy-start | bytes 12292
  70.9 12.7 %copy-start.8 = (f32[128]{0:T(128)S(1)}, f32[128]{0:T(128)}, u32[]{:S(2)}) copy-start(f32[128]{0:T(128)} %param.21) | copy-start | bytes 1540
  97.4 4.5 %copy-start.2 = (bf16[64,16,64]{2,1,0:T(8,128)(2,1)S(1)}, bf16[64,16,64]{2,1,0:T(8,128)(2,1)}, u32[]{:S(2)}) copy-start(bf16[64,16,64]{2,1,0:T(8,128)(2,1)} %fusion.46) | copy-start | bytes 393220
  97.4 4.5 %copy-start.6 = (bf16[64,256]{1,0:T(8,128)(2,1)S(1)}, bf16[64,256]{1,0:T(8,128)(2,1)}, u32[]{:S(2)}) copy-start(bf16[64,256]{1,0:T(8,128)(2,1)} %param.24) | copy-start | bytes 98308
  100.3 3.3 %copy-start.1 = (bf16[64,16,64]{2,1,0:T(8,128)(2,1)S(1)}, bf16[64,16,64]{2,1,0:T(8,128)(2,1)}, u32[]{:S(2)}) copy-start(bf16[64,16,64]{2,1,0:T(8,128)(2,1)} %param.13) | copy-start | bytes 393220
  100.3 3.3 %copy-start.4 = (bf16[256,64]{0,1:T(8,128)(2,1)S(1)}, bf16[256,64]{0,1:T(8,128)(2,1)}, u32[]{:S(2)}) copy-start(bf16[256,64]{0,1:T(8,128)(2,1)} %param.25) | copy-start | bytes 98308
Sparse Core Ops, SparseCore 0:
  11.9 55.2 all-gather.1
where the time goes:
time: 112 us
  matrix products  37.2 us (33%)
  blocking collectives  23.4 us (21%)
  waiting for transfers between devices  22.9 us (20%)
  between operations  14.2 us (13%)
  local copies, waits for them, and re-layouts  7.38 us (7%)
  other arithmetic  6.42 us (6%)
    all_gather x1, blocking collectives, shards(): lax.all_gather(mask_halved, 'row', axis=1, tiled=True)  23.4 us
    all_gather x1, waiting for transfers between devices, shards(): lax.all_gather(normed_input, 'row', axis=1, tiled=True)  22.9 us
    dot_general x1, matrix products, pair_terms(): jnp.einsum('seiz,sje->ijz', folded, right_piece, preferred_element_type=j...  11 us
    dot_general x1, matrix products, shards(): jnp.einsum('hij,sjhc->sihc', weights, heads_piece, preferred_element_type...  7.5 us
    dot_general x1, matrix products, shards(): jnp.einsum('sic,cez->seiz', left_rows, weight_cube, preferred_element_typ...  5.96 us
    dot_general x1, matrix products, shards(): jnp.dot(gathered, content_vector_proj, preferred_element_type=jnp.float32)  4.55 us
    dot_general x1, matrix products, shards(): jnp.dot(gathered, latter_factor_proj, preferred_element_type=jnp.float32)  3.72 us
    transpose x1, local copies, waits for them, and re-layouts, shards(): jnp.einsum('hij,sjhc->sihc', weights, heads_piece, preferred_element_type...  2.87 us
  transfers between devices with their start and end apart: 1, of which 1 were waited for; matrix products, arithmetic and copies ran while one was open for 8% of the time, Pallas kernels for 0%

commit v1 on v0

--- a/solution.py
+++ b/solution.py
@@ -2,6 +2,11 @@
 import jax.numpy as jnp
 from jax import lax
 from jax.sharding import PartitionSpec as P
+
+
+def all_parts(x, mesh_axis, dim):
+    blocks = lax.all_gather(x, mesh_axis)
+    return jnp.concatenate(blocks, axis=dim)
 
 
 def layer_normalize(inputs, gain):
@@ -51,7 +56,7 @@
     head_width = content_vector_proj.shape[1] // head_count
     gathered, gathered_mask = (
         lax.all_gather(normed_input, "row", axis=1, tiled=True),
-        lax.all_gather(mask_halved, "row", axis=1, tiled=True),
+        all_parts(mask_halved, "row", 1),
     )
     right_all = (
         jnp.dot(gathered, latter_factor_proj, preferred_element_type=jnp.float32)

time: 112 us -> 112 us (level)
  transfers between devices with their start and end apart: 1 -> 1, of which waited for: 1 -> 1; matrix products, arithmetic and copies ran while one was open for 8% -> 9% of each run, Pallas kernels for 0% -> 0%
where the time goes in v1:
time: 112 us
  matrix products  37.9 us (34%)
  blocking collectives  23.4 us (21%)
  waiting for transfers between devices  22.2 us (20%)
  between operations  14.2 us (13%)
  local copies, waits for them, and re-layouts  7.38 us (7%)
  other arithmetic  6.42 us (6%)
    all_gather x1, blocking collectives, all_parts(): blocks = lax.all_gather(x, mesh_axis)  23.4 us
    all_gather x1, waiting for transfers between devices, shards(): lax.all_gather(normed_input, 'row', axis=1, tiled=True)  22.2 us
    dot_general x1, matrix products, pair_terms(): jnp.einsum('seiz,sje->ijz', folded, right_piece, preferred_element_type=j...  11 us
    dot_general x1, matrix products, shards(): jnp.einsum('hij,sjhc->sihc', weights, heads_piece, preferred_element_type...  7.5 us
    dot_general x1, matrix products, shards(): jnp.einsum('sic,cez->seiz', left_rows, weight_cube, preferred_element_typ...  5.96 us
    dot_general x1, matrix products, shards(): jnp.dot(gathered, content_vector_proj, preferred_element_type=jnp.float32)  4.55 us
    dot_general x1, matrix products, shards(): jnp.dot(gathered, latter_factor_proj, preferred_element_type=jnp.float32)  3.72 us
    transpose x1, local copies, waits for them, and re-layouts, shards(): jnp.einsum('hij,sjhc->sihc', weights, heads_piece, preferred_element_type...  2.87 us
  transfers between devices with their start and end apart: 1, of which 1 were waited for; matrix products, arithmetic and copies ran while one was open for 9% of the time, Pallas kernels for 0%

profile of v1, /device:TPU:0, one launch (start us, length us, event | category | flops | bytes accessed | tf_op | source)
XLA Modules:
  0.0 111.5 jit_solution(1900197976817647296)
XLA Ops:
  7.2 0.0 copy-start
  7.2 0.0 copy-start.3
  7.2 0.0 all-gather.4.cloned.1.call-start
  7.2 1.2 %convert_reduce_fusion.1 = f32[64,16]{1,0:T(8,128)S(1)} fusion(bf16[64,16,64]{2,1,0:T(8,128)(2,1)} %param.13), kind=kLoop, calls=%fused_computation.44 | loop fusion | flops 130048 | bytes 135168 | tf_op jit(solution)/shard_map/reduce_sum | solution.py:14
  8.4 1.3 %fusion.44 = f32[64,16]{1,0:T(8,128)S(1)} fusion(bf16[64,16,64]{2,1,0:T(8,128)(2,1)} %param.13, f32[64,16]{1,0:T(8,128)S(1)} %broadcast_multiply_fusion), kind=kLoop, calls=%fused_computation.47 | loop fusion | flops 261120 | bytes 139264 | tf_op jit(solution)/shard_map/reduce_sum | solution.py:15
  9.8 2.0 %fusion.46 = bf16[64,16,64]{2,1,0:T(8,128)(2,1)} fusion(bf16[64,16,64]{2,1,0:T(8,128)(2,1)} %param.13, f32[64]{0:T(128)} %param.17, f32[64,16]{1,0:T(8,128)S(1)} %add_rsqrt_fusion, f32[64,16]{1,0:T(8,128)S(1)} %broadcast_multiply_fusion), kind=kLoop, calls=%fused_computation.49 | loop fusion | flops 327680 | bytes 270592 | tf_op jit(solution)/shard_map/convert_element_type | solution.py:40
  11.8 0.0 all-gather.4.cloned.1.call-update
  11.8 0.7 convert_convert_fusion
  12.5 23.4 %all-gather.1 = bf16[16,64,16]{1,2,0:T(8,128)(2,1)S(1)} all-gather(bf16[1,64,16]{1,2,0:T(8,128)(2,1)S(1)} %get-tuple-element.9), channel_id=2, replica_groups=mesh['groups'=2,'row'=16] {'row'}, dimensions={0}, use_global_device_ids=true | all-gather | bytes 34816 | tf_op jit(solution)/shard_map/all_gather | solution.py:8
  35.9 0.1 copy.33
  36.0 1.5 %copy.32 = bf16[16,256,128]{1,2,0:T(8,128)(2,1)S(1)} copy(bf16[16,256,128]{2,1,0:T(8,128)(2,1)} %param.14) | data formatting | bytes 2097152 | tf_op args[1]
  37.5 0.7 broadcast_compare_fusion
  38.2 0.8 convolution_add_fusion.1
  39.0 0.0 copy-done.3
  39.0 6.0 %convert_bitcast_fusion = bf16[64,32,16,128]{3,0,1,2:T(8,128)(2,1)} fusion(bf16[32,32,128]{2,1,0:T(8,128)(2,1)S(1)} %bitcast.65, bf16[64,16,64]{2,1,0:T(8,128)(2,1)} %fusion.46, f32[64,16]{0,1:T(8,128)S(1)} %get-tuple-element.8, bf16[64,32]{0,1:T(8,128)(2,1)} %param.18), kind=kOutput, calls=%fused_computation.6 | convolution fusion | flops 276889600 | bytes 8790016 | tf_op jit(solution)/shard_map/sic,cez->seiz/dot_general | solution.py:52
  45.0 22.2 %all-gather.4.cloned.1.call-done = bf16[64,256,64]{2,1,0:T(8,128)(2,1)} async-done(((bf16[64,16,64]{2,1,0:T(8,128)(2,1)}), bf16[64,256,64]{2,1,0:T(8,128)(2,1)}) %all-gather.4.cloned.1.call-update) | async-done | bytes 2097168 | tf_op jit(solution)/shard_map/all_gather | solution.py:58
  67.2 0.0 copy-done.5
  67.2 3.7 %fusion.19 = bf16[64,256,32,1]{1,2,0,3:T(8,128)(2,1)S(1)} fusion(bf16[64,256,64]{2,1,0:T(8,128)(2,1)} %all-gather.4.cloned.1.call-done, f32[64,256]{1,0:T(8,128)S(1)} %convert_element_type.58, bf16[64,32]{0,1:T(8,128)(2,1)S(1)} %copy-done.5), kind=kOutput, calls=%fused_computation.20 | convolution fusion | flops 68157440 | bytes 3215360 | tf_op jit(solution)/shard_map/dot_general | solution.py:62
  70.9 0.0 copy-start.8
  70.9 11.0 %convert_reduce_fusion = (f32[16,256]{1,0:T(8,128)S(1)}, bf16[16,256,128]{1,2,0:T(8,128)(2,1)S(1)}) fusion(f32[16,256]{1,0:T(8,128)S(1)} %convolution_add_fusion.1, bf16[64,256,32,1]{1,2,0,3:T(8,128)(2,1)S(1)} %fusion.19, bf16[64,32,16,128]{3,0,1,2:T(8,128)(2,1)} %convert_bitcast_fusion, bf16[16,256,128]{1,2,0:T(8,128)(2,1)S(1)} %copy.32), kind=kOutput, calls=%fused_computation.9 | convolution fusion | flops 2150625280 | bytes 11567104 | tf_op jit(solution)/shard_map/seiz,sje->ijz/dot_general | solution.py:20
  82.0 1.3 %copy.43 = bf16[16,256,128]{2,1,0:T(8,128)(2,1)} copy(bf16[16,256,128]{1,2,0:T(8,128)(2,1)S(1)} %get-tuple-element.11) | data formatting | bytes 2097152
  83.3 0.3 fusion.11
  83.7 1.5 %fusion.34 = f32[8,16,256]{2,0,1:T(8,128)S(1)} fusion(bf16[16,256,128]{1,2,0:T(8,128)(2,1)S(1)} %get-tuple-element.11, f32[128]{0:T(128)S(1)} %copy-done.8, f32[16,256]{1,0:T(8,128)S(1)} %add_rsqrt_fusion.1, f32[16,256]{1,0:T(8,128)S(1)} %broadcast_multiply_fusion.1, pred[256]{0:T(512)(128)(4,1)S(1)} %broadcast_compare_fusion, f32[128,8]{0,1:T(8,128)S(1)} %copy-done.7), kind=kOutput, calls=%fused_computation.36 | convolution fusion | flops 52461568 | bytes 1217280 | tf_op jit(solution)/shard_map/ijc,ch->hij/dot_general | solution.py:68
  85.1 0.2 fusion.38
  85.3 4.6 %convolution_convert_fusion = bf16[64,256,256]{1,2,0:T(8,128)(2,1)S(1)} fusion(bf16[64,256,64]{2,1,0:T(8,128)(2,1)} %all-gather.4.cloned.1.call-done, bf16[64,256]{1,0:T(8,128)(2,1)S(1)} %copy-done), kind=kOutput, calls=%fused_computation.7 | convolution fusion | flops 541065216 | bytes 10518528 | tf_op jit(solution)/shard_map/dot_general | solution.py:74
  89.9 7.5 %fusion.8 = f32[64,16,8,32]{3,1,0,2:T(8,128)} fusion(bf16[64,256,8,32]{1,3,2,0:T(8,128)(2,1)S(1)} %bitcast.61, bf16[8,16,256,1]{2,0,1,3:T(8,128)(2,1)S(1)} %fusion.38), kind=kOutput, calls=%fused_computation.12 | convolution fusion | flops 134217728 | bytes 9502720 | tf_op jit(solution)/shard_map/hij,sjhc->sihc/dot_general | solution.py:79
  97.4 2.9 %copy.40 = f32[64,16,8,32]{0,3,2,1:T(8,128)S(1)} copy(f32[64,16,8,32]{3,1,0,2:T(8,128)} %fusion.8) | data formatting | bytes 2097152 | tf_op jit(solution)/shard_map/hij,sjhc->sihc/transpose | solution.py:79
  100.3 0.0 copy-start.1
  100.3 0.0 copy-start.4
  100.3 1.6 %copy.41 = f32[64,16,256]{2,0,1:T(8,128)} copy(f32[64,16,256]{0,2,1:T(8,128)S(1)} %bitcast.62) | data formatting | bytes 2097152 | tf_op jit(solution)/shard_map/reshape | solution.py:80
  101.9 1.6 %fusion.24 = bf16[64,16,256]{2,0,1:T(8,128)(2,1)S(1)} fusion(f32[64,16,256]{2,0,1:T(8,128)} %copy.41, bf16[64,16,64]{2,1,0:T(8,128)(2,1)S(1)} %copy-done.2, bf16[64,256]{1,0:T(8,128)(2,1)S(1)} %copy-done.6), kind=kOutput, calls=%fused_computation.26 | convolution fusion | flops 34865152 | bytes 1736704 | tf_op jit(solution)/shard_map/dot_general | solution.py:82
  103.6 1.1 %fusion.25 = bf16[64,16,64]{2,1,0:T(8,128)(2,1)} fusion(bf16[64,16,64]{2,1,0:T(8,128)(2,1)S(1)} %copy-done.1, bf16[64,16,256]{2,0,1:T(8,128)(2,1)S(1)} %fusion.24, bf16[256,64]{0,1:T(8,128)(2,1)S(1)} %copy-done.4), kind=kOutput, calls=%fused_computation.28 | convolution fusion | flops 33751040 | bytes 819200 | tf_op jit(solution)/shard_map/dot_general | solution.py:85
  (16 shorter events, 0.1 us)
Async XLA Ops:
  7.2 78.2 %copy-start = (bf16[64,256]{1,0:T(8,128)(2,1)S(1)}, bf16[64,256]{1,0:T(8,128)(2,1)}, u32[]{:S(2)}) copy-start(bf16[64,256]{1,0:T(8,128)(2,1)} %param.23) | copy-start | bytes 98308
  7.2 31.8 %copy-start.3 = (bf16[1024,128]{1,0:T(8,128)(2,1)S(1)}, bf16[1024,128]{1,0:T(8,128)(2,1)}, u32[]{:S(2)}) copy-start(bf16[1024,128]{1,0:T(8,128)(2,1)} %param.20) | copy-start | bytes 786436
  7.2 60.0 %all-gather.4.cloned.1.call-start = ((), (), s32[]{:S(2)}) async-start(), calls=%async_computation | async-start | bytes 4456448 | tf_op jit(solution)/shard_map/all_gather | solution.py:58
  39.0 28.2 %copy-start.5 = (bf16[64,32]{0,1:T(8,128)(2,1)S(1)}, bf16[64,32]{0,1:T(8,128)(2,1)}, u32[]{:S(2)}) copy-start(bf16[64,32]{0,1:T(8,128)(2,1)} %param.19) | copy-start | bytes 12292
  70.9 12.7 %copy-start.7 = (f32[128,8]{0,1:T(8,128)S(1)}, f32[128,8]{0,1:T(8,128)}, u32[]{:S(2)}) copy-start(f32[128,8]{0,1:T(8,128)} %param.22) | copy-start | bytes 12292
  70.9 12.7 %copy-start.8 = (f32[128]{0:T(128)S(1)}, f32[128]{0:T(128)}, u32[]{:S(2)}) copy-start(f32[128]{0:T(128)} %param.21) | copy-start | bytes 1540
  97.4 4.5 %copy-start.2 = (bf16[64,16,64]{2,1,0:T(8,128)(2,1)S(1)}, bf16[64,16,64]{2,1,0:T(8,128)(2,1)}, u32[]{:S(2)}) copy-start(bf16[64,16,64]{2,1,0:T(8,128)(2,1)} %fusion.46) | copy-start | bytes 393220
  97.4 4.5 %copy-start.6 = (bf16[64,256]{1,0:T(8,128)(2,1)S(1)}, bf16[64,256]{1,0:T(8,128)(2,1)}, u32[]{:S(2)}) copy-start(bf16[64,256]{1,0:T(8,128)(2,1)} %param.24) | copy-start | bytes 98308
  100.3 3.3 %copy-start.1 = (bf16[64,16,64]{2,1,0:T(8,128)(2,1)S(1)}, bf16[64,16,64]{2,1,0:T(8,128)(2,1)}, u32[]{:S(2)}) copy-start(bf16[64,16,64]{2,1,0:T(8,128)(2,1)} %param.13) | copy-start | bytes 393220
  100.3 3.3 %copy-start.4 = (bf16[256,64]{0,1:T(8,128)(2,1)S(1)}, bf16[256,64]{0,1:T(8,128)(2,1)}, u32[]{:S(2)}) copy-start(bf16[256,64]{0,1:T(8,128)(2,1)} %param.25) | copy-start | bytes 98308
Sparse Core Ops, SparseCore 0:
  11.9 55.2 all-gather.3
